TPU v7x, 512 devices: a whole 4x4x16 slice. The times are simulated.
512 devices in a mesh: segment: 8 (over x, core), frames: 64 (over y, z).
Axes of the slice: x: 4, y: 4, z: 16, core: 2. Of those that a mesh axis runs over, the one named last changes fastest.
Arguments:
- hidden: bfloat16 [8, 16384, 1536], P('segment', 'frames'), may hold values from -3 to 3
- features: bfloat16 [4096, 768], P('frames'), may hold values from -160 to 160, as said below
- kv_weight: bfloat16 [8, 768, 3072], P('segment', None, 'frames'), may hold values from -0.21875 to 0.21875
- mod_table: float32 [8, 32, 3, 1536], P('segment'), may hold values from -4 to 4
- timestep: int32 [8, 256], P('segment', 'frames'), may hold values from 0 to 31
- block_list: int32 [8, 256, 4], P('segment', 'frames'), may hold values from 0 to 63
- block_count: int32 [8, 256], P('segment', 'frames'), may hold values from 1 to 4, as said below
Outputs:
- handed: bfloat16 [8, 16384, 1536], P('segment', 'frames')
Inputs may be any that keep to these rules, and one draw needn't show every extreme that they name: `features`: drawn as normal values, rows may carry common scales; within the bounds given. `block_list`: entry j of a block's list counts when j < the block's count; the others are ignored. `block_count`: the 4 frame blocks of one device have at most 10 live list entries together, and in every section some device has exactly 10.
All inputs are finite; a program needn't handle non-finite values.
Results may differ from a plain program's by a relative error of at most 0.0044.
The roundings to bfloat16 on the way count: a program that leaves them out, or rounds other values in their place, can miss the bound.
Values may be sent and summed in bfloat16 or wider, within the bound.
No kernel may reach another device: no remote copies, remote signals or barrier semaphores. Data moves between devices by JAX's collectives and lax.ppermute only.
A program may use at most 64 MiB of HBM per device.

v0:
```python
import jax
import jax.numpy as jnp
from jax import lax
from jax.sharding import PartitionSpec as P

HEADS = 12
HD = 128
BLK = 64


def from_behind(block, axis, distance):
    devices = range(lax.axis_size(axis))
    route = [((i - distance) % len(devices), i) for i in devices]
    return lax.ppermute(block, axis, route)


def local(hidden, features, kv_weight, mod_table, timestep, block_list, block_count):
    feature_table = lax.all_gather(features, "frames", axis=0, tiled=True)
    stream = hidden[0].astype(jnp.float32)
    tok_rows = stream.shape[0]
    feature_width = stream.shape[1]
    blocks_here = tok_rows // BLK
    normed = stream * lax.rsqrt(jnp.mean(stream * stream, axis=-1, keepdims=True) + 1e-06)
    levels = mod_table.shape[1]
    onehot = (timestep[0][:, None] == jnp.arange(levels, dtype=jnp.int32)[None, :]).astype(
        jnp.float32
    )
    modulate = jnp.sum(onehot[:, :, None, None] * mod_table[0][None], axis=1)
    normed_blocks = normed.reshape(blocks_here, BLK, feature_width)
    queries = (
        normed_blocks * (1.0 + modulate[:, 1][:, None, :]) + modulate[:, 0][:, None, :]
    ).astype(jnp.bfloat16)
    queries = queries.reshape(blocks_here, BLK, HEADS, HD)
    list_counts = block_count[0]
    list_blocks = block_list[0]
    slot_count = list_blocks.shape[1]
    offsets = jnp.arange(BLK, dtype=jnp.int32)
    inv_root = 1.0 / HD**0.5
    row_index = (list_blocks[:, :, None] * BLK + offsets[None, None, :]).reshape(-1)
    key_mask = jnp.repeat(
        jnp.arange(slot_count, dtype=jnp.int32)[None, :] < list_counts[:, None], BLK, axis=1
    )
    selected = jnp.take(feature_table, row_index, axis=0)
    key_values = jnp.dot(
        selected,
        lax.all_gather(kv_weight[0], "frames", axis=1, tiled=True),
        preferred_element_type=jnp.float32,
    ).astype(jnp.bfloat16)
    key_heads = key_values[:, :feature_width].reshape(-1, HEADS, HD)
    value_heads = key_values[:, feature_width:].reshape(-1, HEADS, HD)
    keys_part = key_heads.reshape(blocks_here, -1, HEADS, HD)
    values_part = value_heads.reshape(blocks_here, -1, HEADS, HD)
    scores = jnp.einsum("bqhd,bkhd->bhqk", queries, keys_part, preferred_element_type=jnp.float32)
    softmax_scores = scores
    softmax_scores = jnp.where(
        key_mask[:, None, None, :], softmax_scores * inv_root, jnp.float32(-1e30)
    )
    top_score = jnp.max(softmax_scores, axis=-1, keepdims=True)
    expo = jnp.exp(softmax_scores - top_score)
    weights = (expo / jnp.sum(expo, axis=-1, keepdims=True)).astype(jnp.bfloat16)
    mixed_heads = jnp.einsum(
        "bhqk,bkhd->bqhd", weights, values_part, preferred_element_type=jnp.float32
    )
    part_blocks = blocks_here - 0
    mixed_rows = mixed_heads.reshape(part_blocks * BLK, feature_width)
    gate_rows = jnp.repeat(modulate[0:blocks_here, 2], BLK, axis=0)
    result = (stream + gate_rows * mixed_rows).astype(jnp.bfloat16)
    handed = from_behind(result[None], "segment", 1)
    return handed


def solution(mesh):
    placed = (
        P("segment", "frames", None),
        P("frames", None),
        P("segment", None, "frames"),
        P("segment", None, None, None),
        P("segment", "frames"),
        P("segment", "frames", None),
        P("segment", "frames"),
    )
    return jax.shard_map(
        local, mesh=mesh, in_specs=placed, out_specs=P("segment", "frames", None), check_vma=False
    )
```

profile of v0, /device:TPU:32, one launch (start us, length us, event | category | flops | bytes accessed | tf_op | source)
XLA Modules:
  0.0 365.3 jit_solution(4835332354557125818)
XLA Ops:
  6.5 0.7 all-gather.4.cloned.1.call-update
  7.3 0.7 all-gather.6.cloned.1.call-update
  8.0 0.7 multiply_bitcast_fusion
  8.7 0.1 iota_add_fusion
  8.8 0.1 add.89
  8.9 0.1 add.86
  8.9 1.6 reshape.134
  10.5 0.7 fusion.21
  11.2 0.4 multiply_reduce_fusion
  11.6 0.2 fusion.20
  11.8 0.2 multiply_reduce_fusion.1
  12.1 0.1 rsqrt.12
  12.2 0.1 broadcast_in_dim.41
  12.3 0.1 broadcast_in_dim.42
  12.4 1.4 add_convert_fusion
  13.8 152.8 %all-gather.4.cloned.1.call-done = bf16[4096,768]{1,0:T(8,128)(2,1)} async-done(((bf16[64,768]{1,0:T(8,128)(2,1)}), bf16[4096,768]{1,0:T(8,128)(2,1)}) %all-gather.4.cloned.1.call-update) | async-done | bytes 6291472 | tf_op jit(solution)/shard_map/all_gather | solution.py:18
  166.6 8.1 %gather_fusion = bf16[1024,768]{1,0:T(8,128)(2,1)S(1)} fusion(bf16[4096,768]{1,0:T(8,128)(2,1)} %all-gather.4.cloned.1.call-done, s32[1024]{0:T(1024)S(1)} %broadcast_clamp_fusion), kind=kCustom, calls=%fused_computation | custom fusion | bytes 3149824 | tf_op jit(solution)/shard_map/jit(_take)/gather | solution.py:43
  174.7 137.1 %all-gather.6.cloned.1.call-done = bf16[1,768,3072]{1,2,0:T(8,128)(2,1)} async-done(((bf16[1,768,48]{1,2,0:T(8,128)(2,1)}), bf16[1,768,3072]{1,2,0:T(8,128)(2,1)}) %all-gather.6.cloned.1.call-update) | async-done | bytes 4718608 | tf_op jit(solution)/shard_map/all_gather | solution.py:46
  311.8 7.9 %convolution_convert_fusion = bf16[1024,3072]{1,0:T(8,128)(2,1)S(1)} fusion(bf16[1,768,3072]{1,2,0:T(8,128)(2,1)} %all-gather.6.cloned.1.call-done, bf16[1024,768]{1,0:T(8,128)(2,1)S(1)} %gather_fusion, pred[1024]{0:T(1024)(128)(4,1)S(1)} %compare_and_fusion), kind=kOutput, calls=%fused_computation.2 | convolution fusion | flops 4835770368 | bytes 12583936 | tf_op jit(solution)/shard_map/dot_general | solution.py:44
  319.6 2.2 fusion.25
  321.8 6.9 %reshape.144 = bf16[4,256,12,128]{3,2,1,0:T(8,128)(2,1)} reshape(bf16[1024,1536]{1,0:T(8,128)(2,1)} %get-tuple-element.8) | data formatting | bytes 6291456 | tf_op jit(solution)/shard_map/reshape;reshape | solution.py:52
  328.7 3.6 reshape.145
  332.3 3.7 %fusion.2 = f32[4,12,64,256]{3,2,1,0:T(8,128)S(1)} fusion(bf16[4,256,12,128]{3,2,1,0:T(8,128)(2,1)} %reshape.145, bf16[4,64,12,128]{3,2,1,0:T(8,128)(2,1)} %add_convert_fusion), kind=kOutput, calls=%fused_computation.4 | convolution fusion | flops 201326592 | bytes 7077888 | tf_op jit(solution)/shard_map/bqhd,bkhd->bhqk/dot_general | solution.py:53
  336.1 1.4 fusion.26
  337.5 0.8 copy-done.2
  338.2 2.4 fusion.15
  340.7 0.9 copy.24
  341.6 1.4 reshape.133
  343.0 0.2 broadcast_in_dim.38
  343.2 1.8 fusion.8
  345.0 12.6 %collective-permute-done = bf16[1,256,1536]{2,1,0:T(8,128)(2,1)S(1)} collective-permute-done((bf16[1,256,1536]{2,1,0:T(8,128)(2,1)S(1)}, bf16[1,256,1536]{2,1,0:T(8,128)(2,1)S(1)}, u32[]{:S(2)}, u32[]{:S(2)}) %collective-permute-start) | collective-permute-done | bytes 786464 | tf_op jit(solution)/shard_map/ppermute | solution.py:14
  357.6 0.9 copy.41
  (20 shorter events, 0.2 us)
Async XLA Ops:
  6.5 5.3 %copy-start = (bf16[1,256,1536]{2,1,0:T(8,128)(2,1)S(1)}, bf16[1,256,1536]{2,1,0:T(8,128)(2,1)}, u32[]{:S(2)}) copy-start(bf16[1,256,1536]{2,1,0:T(8,128)(2,1)} %param.7) | copy-start | bytes 2359300
  6.5 4.7 %copy-start.3 = (f32[1,32,3,1536]{3,1,2,0:T(8,128)S(1)}, f32[1,32,3,1536]{3,1,2,0:T(8,128)}, u32[]{:S(2)}) copy-start(f32[1,32,3,1536]{3,1,2,0:T(8,128)} %param.10) | copy-start | bytes 1769476
  6.5 5.6 %copy-start.4 = (s32[1,4]{1,0:T(1,128)S(1)}, s32[1,4]{1,0:T(1,128)}, u32[]{:S(2)}) copy-start(s32[1,4]{1,0:T(1,128)} %param.13) | copy-start | bytes 52
  6.5 160.1 %all-gather.4.cloned.1.call-start = ((), (), s32[]{:S(2)}) async-start(), calls=%async_computation | async-start | bytes 6389760 | tf_op jit(solution)/shard_map/all_gather | solution.py:18
  7.3 304.5 %all-gather.6.cloned.1.call-start = ((), (), s32[]{:S(2)}) async-start(), calls=%async_computation.1 | async-start | bytes 4792320 | tf_op jit(solution)/shard_map/all_gather | solution.py:46
  336.0 2.2 copy-start.2
  341.6 1.6 copy-start.1
  345.0 12.6 %collective-permute-start = (bf16[1,256,1536]{2,1,0:T(8,128)(2,1)S(1)}, bf16[1,256,1536]{2,1,0:T(8,128)(2,1)S(1)}, u32[]{:S(2)}, u32[]{:S(2)}) collective-permute-start(bf16[1,256,1536]{2,1,0:T(8,128)(2,1)S(1)} %fusion.8), channel_id=1, source_target_pairs={{448,0},{0,64},{64,128},{128,192},{192,256},{256,320},{320,384},{3... | collective-permute-start | bytes 2359304 | tf_op jit(solution)/shard_map/ppermute | solution.py:14
Sparse Core Ops, SparseCore 0:
  10.3 156.2 all-gather.3
  169.6 142.1 all-gather.5
where the time goes:
time: 366 us; the launch traced here: 365 us
  waiting for transfers between devices  304 us (83%)
  local copies, waits for them, and re-layouts  26.9 us (7%)
  matrix products  14 us (4%)
  between operations  13.6 us (4%)
  other arithmetic  6.91 us (2%)
    all_gather x1, waiting for transfers between devices, local(): feature_table = lax.all_gather(features, 'frames', axis=0, tiled=True)  153 us
    all_gather x1, waiting for transfers between devices, local(): lax.all_gather(kv_weight[0], 'frames', axis=1, tiled=True)  137 us
    ppermute x1, waiting for transfers between devices, from_behind(): return lax.ppermute(block, axis, route)  12.6 us
    gather x1, local copies, waits for them, and re-layouts, local(): selected = jnp.take(feature_table, row_index, axis=0)  8.07 us
    dot_general x1, matrix products, local(): jnp.dot(selected, lax.all_gather(kv_weight[0], 'frames', axis=1, tiled=Tr...  7.88 us
  transfers between devices with their start and end apart: 3, of which 3 were waited for; matrix products, arithmetic and copies ran while one was open for 4% of the time, Pallas kernels for 0%

commit v1 on v0

--- a/solution.py
+++ b/solution.py
@@ -2,6 +2,7 @@
 import jax.numpy as jnp
 from jax import lax
 from jax.sharding import PartitionSpec as P
+from jax.lax import all_to_all, psum
 
 HEADS = 12
 HD = 128
@@ -41,10 +42,14 @@
         jnp.arange(slot_count, dtype=jnp.int32)[None, :] < list_counts[:, None], BLK, axis=1
     )
     selected = jnp.take(feature_table, row_index, axis=0)
+
+    def try_all_rates(mine_x, shard_axis):
+        return jnp.concatenate(
+            all_to_all(jnp.stack(psum(1, shard_axis) * [mine_x], axis=0), shard_axis, 0, 0), axis=1
+        )
+
     key_values = jnp.dot(
-        selected,
-        lax.all_gather(kv_weight[0], "frames", axis=1, tiled=True),
-        preferred_element_type=jnp.float32,
+        selected, try_all_rates(kv_weight[0], "frames"), preferred_element_type=jnp.float32
     ).astype(jnp.bfloat16)
     key_heads = key_values[:, :feature_width].reshape(-1, HEADS, HD)
     value_heads = key_values[:, feature_width:].reshape(-1, HEADS, HD)

time: 366 us -> 346 us (0.945)
  the two profiles are of different devices: /device:TPU:32 before, /device:TPU:24 now
where the time goes in v1:
time: 346 us
  waiting for transfers between devices  264 us (76%)
  local copies, waits for them, and re-layouts  29.2 us (8%)
  starting transfers between devices  19.1 us (6%)
  matrix products  14 us (4%)
  between operations  13.6 us (4%)
  other arithmetic  5.59 us (2%)
    all_gather x1, waiting for transfers between devices, local(): feature_table = lax.all_gather(features, 'frames', axis=0, tiled=True)  251 us
    all_to_all x1, starting transfers between devices, try_all_rates(): all_to_all(jnp.stack(psum(1, shard_axis) * [mine_x], axis=0), shard_axis,...  19 us
    ppermute x1, waiting for transfers between devices, from_behind(): return lax.ppermute(block, axis, route)  12.6 us
    gather x1, local copies, waits for them, and re-layouts, local(): selected = jnp.take(feature_table, row_index, axis=0)  8.07 us
    dot_general x1, matrix products, local(): jnp.dot(selected, try_all_rates(kv_weight[0], 'frames'), preferred_elemen...  7.9 us
  transfers between devices with their start and end apart: 3, of which 2 were waited for; matrix products, arithmetic and copies ran while one was open for 3% of the time, Pallas kernels for 0%

profile of v1, /device:TPU:24, one launch (start us, length us, event | category | flops | bytes accessed | tf_op | source)
XLA Modules:
  0.0 345.8 jit_solution(13985157988148393152)
XLA Ops:
  6.5 3.4 stack.3
  9.9 19.0 %all-to-all-start = ((bf16[64,768,48]{1,2,0:T(8,128)(2,1)}), bf16[64,768,48]{1,2,0:T(8,128)(2,1)}, u32[]{:S(2)}, u32[]{:S(2)}) async-start(bf16[64,768,48]{1,2,0:T(8,128)(2,1)} %stack.3), calls=%async_computation | async-start | bytes 9437184 | tf_op jit(solution)/shard_map/all_to_all | solution.py:48
  29.0 0.7 all-gather.2.cloned.1.call-update
  29.7 0.1 iota_add_fusion
  29.8 0.1 add.89
  29.9 0.1 add.86
  30.0 0.5 reshape.143
  30.5 0.1 fusion.20
  30.5 0.4 multiply_reduce_fusion
  30.9 0.2 fusion.19
  31.1 0.2 multiply_reduce_fusion.1
  31.3 0.1 rsqrt.12
  31.4 0.1 iota_compare_fusion
  31.5 0.1 broadcast_in_dim.41
  31.6 0.1 broadcast_in_dim.42
  31.7 1.4 add_convert_fusion
  33.1 251.0 %all-gather.2.cloned.1.call-done = bf16[4096,768]{1,0:T(8,128)(2,1)} async-done(((bf16[64,768]{1,0:T(8,128)(2,1)}), bf16[4096,768]{1,0:T(8,128)(2,1)}) %all-gather.2.cloned.1.call-update) | async-done | bytes 6291472 | tf_op jit(solution)/shard_map/all_gather | solution.py:19
  284.1 8.1 %gather_fusion = bf16[1024,768]{1,0:T(8,128)(2,1)S(1)} fusion(bf16[4096,768]{1,0:T(8,128)(2,1)} %all-gather.2.cloned.1.call-done, s32[1024]{0:T(1024)S(1)} %broadcast_clamp_fusion), kind=kCustom, calls=%fused_computation | custom fusion | bytes 3149824 | tf_op jit(solution)/shard_map/jit(_take)/gather | solution.py:44
  292.2 7.9 %convolution_convert_fusion = bf16[1024,3072]{1,0:T(8,128)(2,1)S(1)} fusion(bf16[768,3072]{0,1:T(8,128)(2,1)} %bitcast.7, bf16[1024,768]{1,0:T(8,128)(2,1)S(1)} %gather_fusion, pred[1024]{0:T(1024)(128)(4,1)S(1)} %compare_and_fusion), kind=kOutput, calls=%fused_computation.2 | convolution fusion | flops 4835770368 | bytes 12583936 | tf_op jit(solution)/shard_map/dot_general | solution.py:51
  300.1 2.2 fusion.24
  302.3 6.9 %reshape.152 = bf16[4,256,12,128]{3,2,1,0:T(8,128)(2,1)} reshape(bf16[1024,1536]{1,0:T(8,128)(2,1)} %get-tuple-element.8) | data formatting | bytes 6291456 | tf_op jit(solution)/shard_map/reshape;reshape | solution.py:57
  309.1 3.6 %reshape.153 = bf16[4,256,12,128]{3,2,1,0:T(8,128)(2,1)} reshape(bf16[1024,1536]{1,0:T(8,128)(2,1)S(1)} %get-tuple-element.7) | data formatting | bytes 6291456 | tf_op jit(solution)/shard_map/reshape;reshape | solution.py:56
  312.8 3.7 %fusion.1 = f32[4,12,64,256]{3,2,1,0:T(8,128)S(1)} fusion(bf16[4,256,12,128]{3,2,1,0:T(8,128)(2,1)} %reshape.153, bf16[4,64,12,128]{3,2,1,0:T(8,128)(2,1)} %add_convert_fusion), kind=kOutput, calls=%fused_computation.3 | convolution fusion | flops 201326592 | bytes 7077888 | tf_op jit(solution)/shard_map/bqhd,bkhd->bhqk/dot_general | solution.py:58
  316.5 1.4 fusion.25
  317.9 0.8 copy-done.2
  318.7 2.4 fusion.14
  321.1 0.9 copy.25
  322.1 1.4 reshape.142
  323.4 0.2 broadcast_in_dim.38
  323.6 1.8 fusion.7
  325.4 12.6 %collective-permute-done = bf16[1,256,1536]{2,1,0:T(8,128)(2,1)S(1)} collective-permute-done((bf16[1,256,1536]{2,1,0:T(8,128)(2,1)S(1)}, bf16[1,256,1536]{2,1,0:T(8,128)(2,1)S(1)}, u32[]{:S(2)}, u32[]{:S(2)}) %collective-permute-start) | collective-permute-done | bytes 786464 | tf_op jit(solution)/shard_map/ppermute | solution.py:15
  338.1 0.9 copy.42
  (24 shorter events, 0.2 us)
Async XLA Ops:
  9.9 19.8 %copy-start.4 = (s32[1,4,4]{2,1,0:T(4,128)S(1)}, s32[1,4,4]{2,1,0:T(4,128)}, u32[]{:S(2)}) copy-start(s32[1,4,4]{2,1,0:T(4,128)} %param.12) | copy-start | bytes 196
  9.9 20.0 %copy-start = (bf16[1,256,1536]{2,1,0:T(8,128)(2,1)S(1)}, bf16[1,256,1536]{2,1,0:T(8,128)(2,1)}, u32[]{:S(2)}) copy-start(bf16[1,256,1536]{2,1,0:T(8,128)(2,1)} %param.7) | copy-start | bytes 2359300
  9.9 20.5 %copy-start.5 = (s32[1,4]{1,0:T(1,128)S(1)}, s32[1,4]{1,0:T(1,128)}, u32[]{:S(2)}) copy-start(s32[1,4]{1,0:T(1,128)} %param.11) | copy-start | bytes 52
  9.9 282.2 %all-to-all-start = ((bf16[64,768,48]{1,2,0:T(8,128)(2,1)}), bf16[64,768,48]{1,2,0:T(8,128)(2,1)}, u32[]{:S(2)}, u32[]{:S(2)}) async-start(bf16[64,768,48]{1,2,0:T(8,128)(2,1)} %stack.3), calls=%async_computation | async-start | bytes 9437184 | tf_op jit(solution)/shard_map/all_to_all | solution.py:48
  28.9 1.6 copy-start.3
  29.0 2.5 copy-start.6
  29.0 255.1 %all-gather.2.cloned.1.call-start = ((), (), s32[]{:S(2)}) async-start(), calls=%async_computation.1 | async-start | bytes 6389760 | tf_op jit(solution)/shard_map/all_gather | solution.py:19
  316.5 2.2 copy-start.2
  322.0 1.6 copy-start.1
  325.4 12.6 %collective-permute-start = (bf16[1,256,1536]{2,1,0:T(8,128)(2,1)S(1)}, bf16[1,256,1536]{2,1,0:T(8,128)(2,1)S(1)}, u32[]{:S(2)}, u32[]{:S(2)}) collective-permute-start(bf16[1,256,1536]{2,1,0:T(8,128)(2,1)S(1)} %fusion.7), channel_id=1, source_target_pairs={{448,0},{0,64},{64,128},{128,192},{192,256},{256,320},{320,384},{3... | collective-permute-start | bytes 2359304 | tf_op jit(solution)/shard_map/ppermute | solution.py:15
Sparse Core Ops, SparseCore 0:
  32.8 251.2 all-gather.1
